TPU v7x, 32 devices: a whole 2x2x4 slice. The times are simulated.
32 devices in a mesh: blk: 16 (over z, y, x), grp: 2 (over core).
Axes of the slice: x: 2, y: 2, z: 4, core: 2. Of those that a mesh axis runs over, the one named last changes fastest.
Arguments:
- schur_blocks: bfloat16 [64, 1024, 1024], P(('blk', 'grp')), may hold values from -1 to 5, as said below
- residual: float32 [64, 1024, 128], P(('blk', 'grp')), may hold values from -200 to 200
- direction: float32 [64, 1024, 128], P(('blk', 'grp')), may hold values from -200 to 200
- corner_map: int32 [64, 24], P(('blk', 'grp')), may hold values from 0 to 511
- panel_order: int32 [8], replicated, may hold values from 0 to 7, each once
- coarse_factor: float32 [8, 8, 1024, 1024], P(None, None, 'blk'), may hold values from -0.0625 to 0.0625
- block_inverses: float32 [8, 1024, 1024], P(None, 'blk'), may hold values from -0.1875 to 0.1875
Outputs:
- residual_next: float32 [64, 1024, 128], P(('blk', 'grp'))
- direction_next: float32 [64, 1024, 128], P(('blk', 'grp'))
Inputs may be any that keep to these rules, and one draw needn't show every extreme that they name: `schur_blocks`: each subdomain's block is symmetric positive definite. `panel_order`: each coarse block appears once.
All inputs are finite; a program needn't handle non-finite values.
Results may differ from a plain program's by a relative error of at most 0.0048.
Values sent between devices are 32-bit elements; how exact they have to be, the bound alone decides.
No kernel may reach another device: no remote copies, remote signals or barrier semaphores. Data moves between devices by JAX's collectives and lax.ppermute only.
A program may use at most 64 MiB of HBM per device.

v0:
```python
import jax
import jax.numpy as jnp
from jax import lax
from jax.sharding import PartitionSpec as P

PANELS = 8
precise = lax.Precision.HIGHEST


def squares(residual):
    return lax.psum(jnp.sum(residual * residual, axis=(0, 1)), ("blk", "grp"))


def solve(coarse, panel_order, coarse_factor, block_inverses):
    pending = jnp.zeros_like(coarse)
    solved = jnp.zeros_like(coarse)
    for position in range(PANELS):
        current = panel_order[position]
        target = lax.dynamic_index_in_dim(coarse - pending, current, 0, keepdims=False)
        inverse = lax.dynamic_index_in_dim(block_inverses, current, 0, keepdims=False)
        block_value = jnp.dot(
            inverse,
            lax.all_gather(target, "blk", axis=0, tiled=True),
            precision=precise,
            preferred_element_type=jnp.float32,
        )
        solved = lax.dynamic_update_index_in_dim(solved, block_value, current, 0)
        if position + 1 < PANELS:
            coupling = lax.dynamic_index_in_dim(coarse_factor, current, 1, keepdims=False)
            pending = pending + jnp.einsum(
                "aic,cv->aiv",
                coupling,
                lax.all_gather(block_value, "blk", axis=0, tiled=True),
                precision=precise,
            )
    return solved


def local(
    schur_blocks, residual, direction, corner_map, panel_order, coarse_factor, block_inverses
):
    panels = block_inverses.shape[0]
    rows_b = block_inverses.shape[1]
    sub_count = schur_blocks.shape[0]
    corners = corner_map.shape[1]
    columns_iota = lax.broadcasted_iota(jnp.int32, (sub_count, corners, panels * rows_b), 2)
    placing = (corner_map[:, :, None] == columns_iota).astype(jnp.float32)
    norm_now = squares(residual)
    applied = jnp.einsum(
        "sij,sjv->siv",
        schur_blocks,
        direction.astype(jnp.bfloat16),
        preferred_element_type=jnp.float32,
    )
    curvature = lax.psum(jnp.sum(direction * applied, axis=(0, 1)), ("blk", "grp"))
    step_size = norm_now / curvature
    residual = residual - step_size * applied
    norm_next = squares(residual)
    corner_part = jnp.einsum("scm,scv->mv", placing, residual[:, :corners, :], precision=precise)
    corner_part = corner_part.reshape(panels, rows_b, -1)
    coarse_part = lax.psum(corner_part, "grp")
    solved = solve(coarse_part, panel_order, coarse_factor, block_inverses)
    flat_solved = solved.reshape(panels * rows_b, -1)
    correction = jnp.einsum("scm,mv->scv", placing, flat_solved, precision=precise)
    corrected = jnp.concatenate(
        [residual[:, :corners, :] + correction, residual[:, corners:, :]], axis=1
    )
    direction = corrected + norm_next / norm_now * direction
    return (residual, direction)


def solution(mesh):
    in_specs = (
        P(("blk", "grp"), None, None),
        P(("blk", "grp"), None, None),
        P(("blk", "grp"), None, None),
        P(("blk", "grp"), None),
        P(),
        P(None, None, "blk", None),
        P(None, "blk", None),
    )
    out_specs = (P(("blk", "grp"), None, None), P(("blk", "grp"), None, None))
    return jax.shard_map(local, mesh=mesh, in_specs=in_specs, out_specs=out_specs, check_vma=False)
```

profile of v0, /device:TPU:0, one launch (start us, length us, event | category | flops | bytes accessed | tf_op | source)
XLA Modules:
  0.0 743.4 jit_solution(7819238958384494164)
XLA Ops:
  7.2 0.0 copy-start
  7.2 0.0 all-reduce.3.cloned.1.call-start
  7.2 1.6 multiply_reduce_fusion.2
  8.9 5.0 multiply_reduce_fusion.1
  13.9 0.0 copy-start.7
  13.9 0.0 copy-start.6
  13.9 41.9 %all-reduce = (f32[128]{0:T(128)S(1)}, f32[128]{0:T(128)S(1)}) all-reduce(f32[128]{0:T(128)S(1)} %multiply_reduce_fusion.2, f32[128]{0:T(128)S(1)} %get-tuple-element.14), channel_id=1, replica_groups=mesh['blk'=16,'grp'=2] {'blk','grp'}, use_global_device_ids=true, to_apply=%region_1.0 | all-reduce | flops 256 | bytes 2048 | tf_op jit(solution)/shard_map/psum | solution.py:11
  55.8 1.8 multiply_reduce_fusion
  57.6 0.0 copy-start.2
  57.7 0.0 copy-done.7
  57.7 1.2 fusion.77
  58.8 0.0 all-reduce.3.cloned.1.call-update
  58.9 0.0 copy-done.6
  58.9 0.7 fusion.96
  69.5 1.0 slice.42
  70.6 40.0 %psum.31 = f32[128]{0:T(128)S(1)} all-reduce(f32[128]{0:T(128)S(1)} %get-tuple-element.4), channel_id=1, replica_groups=mesh['blk'=16,'grp'=2] {'blk','grp'}, use_global_device_ids=true, to_apply=%region_6.0 | all-reduce | flops 128 | bytes 1024 | tf_op jit(solution)/shard_map/psum | solution.py:11
  115.6 0.0 all-reduce.3.cloned.1.call-done
  115.7 0.8 constant_dynamic-slice_fusion
  116.4 43.7 %all-gather = f32[1,1024,128]{2,1,0:T(8,128)S(1)} all-gather(f32[1,64,128]{2,1,0:T(8,128)S(1)} %constant_dynamic-slice_fusion), channel_id=2, replica_groups=mesh['blk'=16,'grp'=2] {'blk'}, dimensions={1}, use_global_device_ids=true | all-gather | bytes 557056 | tf_op jit(solution)/shard_map/all_gather | solution.py:23
  160.2 0.0 copy-start.5
  160.2 0.0 copy-done
  160.2 0.0 copy-start.1
  160.2 0.5 bitcast_dynamic-update-slice_fusion.6
  160.7 38.5 %all_gather.46 = f32[1024,128]{1,0:T(8,128)S(1)} all-gather(f32[64,128]{1,0:T(8,128)S(1)} %get-tuple-element.17), channel_id=1, replica_groups=mesh['blk'=16,'grp'=2] {'blk'}, dimensions={0}, use_global_device_ids=true | all-gather | bytes 557056 | tf_op jit(solution)/shard_map/all_gather | solution.py:33
  199.2 3.4 fusion.12
  202.6 0.0 copy-done.5
  202.6 40.7 %all-gather.1 = f32[1,1024,128]{2,1,0:T(8,128)S(1)} all-gather(f32[1,64,128]{2,1,0:T(8,128)S(1)} %dynamic-slice_subtract_fusion.6), channel_id=3, replica_groups=mesh['blk'=16,'grp'=2] {'blk'}, dimensions={1}, use_global_device_ids=true | all-gather | bytes 557056 | tf_op jit(solution)/shard_map/all_gather | solution.py:23
  243.3 0.5 bitcast_dynamic-update-slice_fusion.5
  243.8 38.6 %all_gather.48 = f32[1024,128]{1,0:T(8,128)S(1)} all-gather(f32[64,128]{1,0:T(8,128)S(1)} %get-tuple-element.19), channel_id=1, replica_groups=mesh['blk'=16,'grp'=2] {'blk'}, dimensions={0}, use_global_device_ids=true | all-gather | bytes 557056 | tf_op jit(solution)/shard_map/all_gather | solution.py:33
  282.4 3.4 fusion.21
  285.8 40.3 %all-gather.2 = f32[1,1024,128]{2,1,0:T(8,128)S(1)} all-gather(f32[1,64,128]{2,1,0:T(8,128)S(1)} %dynamic-slice_subtract_fusion.5), channel_id=4, replica_groups=mesh['blk'=16,'grp'=2] {'blk'}, dimensions={1}, use_global_device_ids=true | all-gather | bytes 557056 | tf_op jit(solution)/shard_map/all_gather | solution.py:23
  326.1 0.5 bitcast_dynamic-update-slice_fusion.4
  326.6 38.6 %all_gather.50 = f32[1024,128]{1,0:T(8,128)S(1)} all-gather(f32[64,128]{1,0:T(8,128)S(1)} %get-tuple-element.21), channel_id=1, replica_groups=mesh['blk'=16,'grp'=2] {'blk'}, dimensions={0}, use_global_device_ids=true | all-gather | bytes 557056 | tf_op jit(solution)/shard_map/all_gather | solution.py:33
  365.2 3.4 fusion.24
  368.6 41.1 %all-gather.3 = f32[1,1024,128]{2,1,0:T(8,128)S(1)} all-gather(f32[1,64,128]{2,1,0:T(8,128)S(1)} %dynamic-slice_subtract_fusion.4), channel_id=5, replica_groups=mesh['blk'=16,'grp'=2] {'blk'}, dimensions={1}, use_global_device_ids=true | all-gather | bytes 557056 | tf_op jit(solution)/shard_map/all_gather | solution.py:23
  409.8 0.5 bitcast_dynamic-update-slice_fusion.3
  410.2 38.3 %all_gather.52 = f32[1024,128]{1,0:T(8,128)S(1)} all-gather(f32[64,128]{1,0:T(8,128)S(1)} %get-tuple-element.23), channel_id=1, replica_groups=mesh['blk'=16,'grp'=2] {'blk'}, dimensions={0}, use_global_device_ids=true | all-gather | bytes 557056 | tf_op jit(solution)/shard_map/all_gather | solution.py:33
  448.5 0.0 copy-done.1
  448.5 1.8 fusion.27
  450.3 40.8 %all-gather.4 = f32[1,1024,128]{2,1,0:T(8,128)S(1)} all-gather(f32[1,64,128]{2,1,0:T(8,128)S(1)} %dynamic-slice_subtract_fusion.3), channel_id=6, replica_groups=mesh['blk'=16,'grp'=2] {'blk'}, dimensions={1}, use_global_device_ids=true | all-gather | bytes 557056 | tf_op jit(solution)/shard_map/all_gather | solution.py:23
  491.1 0.5 bitcast_dynamic-update-slice_fusion.2
  491.6 38.6 %all_gather.54 = f32[1024,128]{1,0:T(8,128)S(1)} all-gather(f32[64,128]{1,0:T(8,128)S(1)} %get-tuple-element.25), channel_id=1, replica_groups=mesh['blk'=16,'grp'=2] {'blk'}, dimensions={0}, use_global_device_ids=true | all-gather | bytes 557056 | tf_op jit(solution)/shard_map/all_gather | solution.py:33
  530.2 1.8 fusion.30
  532.0 40.5 %all-gather.5 = f32[1,1024,128]{2,1,0:T(8,128)S(1)} all-gather(f32[1,64,128]{2,1,0:T(8,128)S(1)} %dynamic-slice_subtract_fusion.2), channel_id=7, replica_groups=mesh['blk'=16,'grp'=2] {'blk'}, dimensions={1}, use_global_device_ids=true | all-gather | bytes 557056 | tf_op jit(solution)/shard_map/all_gather | solution.py:23
  572.5 0.4 bitcast_dynamic-update-slice_fusion.1
  573.0 38.5 %all_gather.56 = f32[1024,128]{1,0:T(8,128)S(1)} all-gather(f32[64,128]{1,0:T(8,128)S(1)} %get-tuple-element.27), channel_id=1, replica_groups=mesh['blk'=16,'grp'=2] {'blk'}, dimensions={0}, use_global_device_ids=true | all-gather | bytes 557056 | tf_op jit(solution)/shard_map/all_gather | solution.py:33
  611.4 1.8 fusion.33
  613.3 40.4 %all-gather.6 = f32[1,1024,128]{2,1,0:T(8,128)S(1)} all-gather(f32[1,64,128]{2,1,0:T(8,128)S(1)} %dynamic-slice_subtract_fusion.1), channel_id=8, replica_groups=mesh['blk'=16,'grp'=2] {'blk'}, dimensions={1}, use_global_device_ids=true | all-gather | bytes 557056 | tf_op jit(solution)/shard_map/all_gather | solution.py:23
  653.6 0.5 bitcast_dynamic-update-slice_fusion
  654.1 38.3 %all_gather.58 = f32[1024,128]{1,0:T(8,128)S(1)} all-gather(f32[64,128]{1,0:T(8,128)S(1)} %get-tuple-element.29), channel_id=1, replica_groups=mesh['blk'=16,'grp'=2] {'blk'}, dimensions={0}, use_global_device_ids=true | all-gather | bytes 557056 | tf_op jit(solution)/shard_map/all_gather | solution.py:33
  692.4 0.0 copy-start.3
  692.4 0.0 copy-start.4
  692.4 1.8 fusion
  694.2 40.5 %all-gather.7 = f32[1,1024,128]{2,1,0:T(8,128)S(1)} all-gather(f32[1,64,128]{2,1,0:T(8,128)S(1)} %dynamic-slice_subtract_fusion), channel_id=9, replica_groups=mesh['blk'=16,'grp'=2] {'blk'}, dimensions={1}, use_global_device_ids=true | all-gather | bytes 557056 | tf_op jit(solution)/shard_map/all_gather | solution.py:23
  734.7 0.5 fusion.36
  735.2 0.0 copy-done.2
  735.2 0.2 convolution_add_fusion
  735.4 0.0 copy-done.3
  735.4 0.0 copy-done.4
  735.4 1.1 maximum_add_fusion
  (10 shorter events, 0.1 us)
Async XLA Ops:
  7.2 153.0 %copy-start = (f32[8,64,1024]{2,1,0:T(8,128)S(1)}, f32[8,64,1024]{2,1,0:T(8,128)}, u32[]{:S(2)}) copy-start(f32[8,64,1024]{2,1,0:T(8,128)} %param.13) | copy-start | bytes 6291460
  7.2 108.5 %all-reduce.3.cloned.1.call-start = ((), (), s32[]{:S(2)}) async-start(), calls=%async_computation | async-start | bytes 524288 | tf_op jit(solution)/shard_map/psum | solution.py:61
  13.9 43.8 %copy-start.7 = (s32[2,24]{1,0:T(2,128)S(1)}, s32[2,24]{1,0:T(2,128)}, u32[]{:S(2)}) copy-start(s32[2,24]{1,0:T(2,128)} %param.10) | copy-start | bytes 580
  13.9 45.0 %copy-start.6 = (s32[8]{0:T(128)S(1)}, s32[8]{0:T(128)}, u32[]{:S(2)}) copy-start(s32[8]{0:T(128)} %param.11) | copy-start | bytes 100
  57.6 677.5 %copy-start.2 = (f32[2,1024,128]{2,1,0:T(8,128)}, f32[2,1024,128]{2,1,0:T(8,128)S(1)}, u32[]{:S(2)}) copy-start(f32[2,1024,128]{2,1,0:T(8,128)S(1)} %get-tuple-element.5) | copy-start | bytes 3145732
  160.2 42.4 %copy-start.5 = (f32[8,64,128]{2,1,0:T(8,128)S(1)}, f32[8,64,128]{2,1,0:T(8,128)}, u32[]{:S(2)}) copy-start(f32[8,64,128]{2,1,0:T(8,128)} %all-reduce.3.cloned.1.call-done) | copy-start | bytes 786436
  160.2 288.3 %copy-start.1 = (f32[8,8,64,1024]{3,2,1,0:T(8,128)S(1)}, f32[8,8,64,1024]{3,2,1,0:T(8,128)}, u32[]{:S(2)}) copy-start(f32[8,8,64,1024]{3,2,1,0:T(8,128)} %param.12) | copy-start | bytes 50331652
  692.4 43.1 %copy-start.3 = (f32[2,1024,128]{2,1,0:T(8,128)S(1)}, f32[2,1024,128]{2,1,0:T(8,128)}, u32[]{:S(2)}) copy-start(f32[2,1024,128]{2,1,0:T(8,128)} %param.9) | copy-start | bytes 3145732
  692.4 43.1 %copy-start.4 = (f32[2,1000,128]{2,1,0:T(8,128)S(1)}, f32[2,1000,128]{2,1,0:T(8,128)}, u32[]{:S(2)}) copy-start(f32[2,1000,128]{2,1,0:T(8,128)} %slice.42) | copy-start | bytes 3072004
Sparse Core Ops, SparseCore 0:
  59.0 18.0 all-reduce.2
where the time goes:
time: 744 us; the launch traced here: 743 us
  blocking collectives  679 us (91%)
  between operations  29.3 us (4%)
  matrix products  27.4 us (4%)
    all_gather x8, blocking collectives, solve(): lax.all_gather(target, 'blk', axis=0, tiled=True)  328 us
    all_gather x7, blocking collectives, solve(): lax.all_gather(block_value, 'blk', axis=0, tiled=True)  269 us
    psum x2, blocking collectives, squares(): return lax.psum(jnp.sum(residual * residual, axis=(0, 1)), ('blk', 'grp'))  82 us
    dot_general x7, matrix products, solve(): jnp.einsum('aic,cv->aiv', coupling, lax.all_gather(block_value, 'blk', ax...  17.4 us
  transfers between devices with their start and end apart: 1, of which 0 were waited for; matrix products, arithmetic and copies ran while one was open for 0% of the time, Pallas kernels for 0%

commit v1 on v0

--- a/solution.py
+++ b/solution.py
@@ -7,8 +7,13 @@
 precise = lax.Precision.HIGHEST
 
 
+def one_after_other(x, inner_axis, outer_axis):
+    partial = lax.psum(x, inner_axis)
+    return lax.psum(partial, outer_axis)
+
+
 def squares(residual):
-    return lax.psum(jnp.sum(residual * residual, axis=(0, 1)), ("blk", "grp"))
+    return one_after_other(jnp.sum(residual * residual, axis=(0, 1)), "grp", "blk")
 
 
 def solve(coarse, panel_order, coarse_factor, block_inverses):

time: 744 us -> 783 us (1.052)
  blocking collectives: 679 us -> 718 us
    psum x2 -> x5, blocking collectives: 82 us -> 125 us  [the longest x2 83.3 us: one_after_other(): return lax.psum(partial, outer_axis)]
    all_gather x8, blocking collectives: 328 us -> 308 us  [solve(): lax.all_gather(target, 'blk', axis=0, tiled=True)]
    all_gather x7, blocking collectives: 269 us -> 285 us  [solve(): lax.all_gather(block_value, 'blk', axis=0, tiled=True)]
where the time goes in v1:
time: 783 us; the launch traced here: 782 us
  blocking collectives  718 us (92%)
  between operations  29.2 us (4%)
  matrix products  27.4 us (3%)
    all_gather x8, blocking collectives, solve(): lax.all_gather(target, 'blk', axis=0, tiled=True)  308 us
    all_gather x7, blocking collectives, solve(): lax.all_gather(block_value, 'blk', axis=0, tiled=True)  285 us
    psum x2, blocking collectives, one_after_other(): return lax.psum(partial, outer_axis)  83.3 us
    psum x1, blocking collectives, local(): lax.psum(jnp.sum(direction * applied, axis=(0, 1)), ('blk', 'grp'))  36.8 us
    dot_general x7, matrix products, solve(): jnp.einsum('aic,cv->aiv', coupling, lax.all_gather(block_value, 'blk', ax...  17.4 us
  transfers between devices with their start and end apart: 1, of which 0 were waited for; matrix products, arithmetic and copies ran while one was open for 0% of the time, Pallas kernels for 0%

profile of v1, /device:TPU:0, one launch (start us, length us, event | category | flops | bytes accessed | tf_op | source)
XLA Modules:
  0.0 781.9 jit_solution(6791802455828723292)
XLA Ops:
  7.2 0.0 copy-start
  7.2 0.0 all-reduce.2.cloned.1.call-start
  7.2 1.6 multiply_reduce_fusion.2
  8.9 2.6 psum.42
  11.5 43.3 %psum.43 = f32[128]{0:T(128)S(1)} all-reduce(f32[128]{0:T(128)S(1)} %psum.42), channel_id=1, replica_groups=mesh['blk'=16,'grp'=2] {'blk'}, use_global_device_ids=true, to_apply=%region_2.0 | all-reduce | flops 128 | bytes 1024 | tf_op jit(solution)/shard_map/psum | solution.py:12
  54.8 5.0 multiply_reduce_fusion.1
  59.8 0.0 copy-start.7
  59.8 0.0 copy-start.6
  59.8 36.8 %psum.44 = f32[128]{0:T(128)S(1)} all-reduce(f32[128]{0:T(128)S(1)} %get-tuple-element.12), channel_id=1, replica_groups=mesh['blk'=16,'grp'=2] {'blk','grp'}, use_global_device_ids=true, to_apply=%region_4.0 | all-reduce | flops 128 | bytes 1024 | tf_op jit(solution)/shard_map/psum | solution.py:60
  96.6 1.8 multiply_reduce_fusion
  98.5 0.0 copy-start.2
  98.5 0.0 copy-done.7
  98.5 1.2 fusion.77
  99.6 0.0 all-reduce.2.cloned.1.call-update
  99.7 0.0 copy-done.6
  99.7 0.7 fusion.96
  110.3 1.0 slice.42
  111.4 2.4 psum.46
  113.8 40.0 %psum.47 = f32[128]{0:T(128)S(1)} all-reduce(f32[128]{0:T(128)S(1)} %psum.46), channel_id=1, replica_groups=mesh['blk'=16,'grp'=2] {'blk'}, use_global_device_ids=true, to_apply=%region_8.0 | all-reduce | flops 128 | bytes 1024 | tf_op jit(solution)/shard_map/psum | solution.py:12
  158.8 0.0 all-reduce.2.cloned.1.call-done
  158.8 0.8 constant_dynamic-slice_fusion
  159.6 38.6 %all-gather = f32[1,1024,128]{2,1,0:T(8,128)S(1)} all-gather(f32[1,64,128]{2,1,0:T(8,128)S(1)} %constant_dynamic-slice_fusion), channel_id=2, replica_groups=mesh['blk'=16,'grp'=2] {'blk'}, dimensions={1}, use_global_device_ids=true | all-gather | bytes 557056 | tf_op jit(solution)/shard_map/all_gather | solution.py:28
  198.2 0.0 copy-start.5
  198.2 0.0 copy-done
  198.2 0.0 copy-start.1
  198.2 0.5 bitcast_dynamic-update-slice_fusion.6
  198.7 40.8 %all_gather.46 = f32[1024,128]{1,0:T(8,128)S(1)} all-gather(f32[64,128]{1,0:T(8,128)S(1)} %get-tuple-element.15), channel_id=1, replica_groups=mesh['blk'=16,'grp'=2] {'blk'}, dimensions={0}, use_global_device_ids=true | all-gather | bytes 557056 | tf_op jit(solution)/shard_map/all_gather | solution.py:38
  239.5 3.4 fusion.12
  242.9 0.0 copy-done.5
  242.9 38.4 %all-gather.1 = f32[1,1024,128]{2,1,0:T(8,128)S(1)} all-gather(f32[1,64,128]{2,1,0:T(8,128)S(1)} %dynamic-slice_subtract_fusion.6), channel_id=3, replica_groups=mesh['blk'=16,'grp'=2] {'blk'}, dimensions={1}, use_global_device_ids=true | all-gather | bytes 557056 | tf_op jit(solution)/shard_map/all_gather | solution.py:28
  281.3 0.5 bitcast_dynamic-update-slice_fusion.5
  281.8 40.5 %all_gather.48 = f32[1024,128]{1,0:T(8,128)S(1)} all-gather(f32[64,128]{1,0:T(8,128)S(1)} %get-tuple-element.17), channel_id=1, replica_groups=mesh['blk'=16,'grp'=2] {'blk'}, dimensions={0}, use_global_device_ids=true | all-gather | bytes 557056 | tf_op jit(solution)/shard_map/all_gather | solution.py:38
  322.3 3.4 fusion.21
  325.7 38.5 %all-gather.2 = f32[1,1024,128]{2,1,0:T(8,128)S(1)} all-gather(f32[1,64,128]{2,1,0:T(8,128)S(1)} %dynamic-slice_subtract_fusion.5), channel_id=4, replica_groups=mesh['blk'=16,'grp'=2] {'blk'}, dimensions={1}, use_global_device_ids=true | all-gather | bytes 557056 | tf_op jit(solution)/shard_map/all_gather | solution.py:28
  364.2 0.5 bitcast_dynamic-update-slice_fusion.4
  364.6 40.7 %all_gather.50 = f32[1024,128]{1,0:T(8,128)S(1)} all-gather(f32[64,128]{1,0:T(8,128)S(1)} %get-tuple-element.19), channel_id=1, replica_groups=mesh['blk'=16,'grp'=2] {'blk'}, dimensions={0}, use_global_device_ids=true | all-gather | bytes 557056 | tf_op jit(solution)/shard_map/all_gather | solution.py:38
  405.3 3.4 fusion.24
  408.7 38.6 %all-gather.3 = f32[1,1024,128]{2,1,0:T(8,128)S(1)} all-gather(f32[1,64,128]{2,1,0:T(8,128)S(1)} %dynamic-slice_subtract_fusion.4), channel_id=5, replica_groups=mesh['blk'=16,'grp'=2] {'blk'}, dimensions={1}, use_global_device_ids=true | all-gather | bytes 557056 | tf_op jit(solution)/shard_map/all_gather | solution.py:28
  447.4 0.5 bitcast_dynamic-update-slice_fusion.3
  447.8 41.1 %all_gather.52 = f32[1024,128]{1,0:T(8,128)S(1)} all-gather(f32[64,128]{1,0:T(8,128)S(1)} %get-tuple-element.21), channel_id=1, replica_groups=mesh['blk'=16,'grp'=2] {'blk'}, dimensions={0}, use_global_device_ids=true | all-gather | bytes 557056 | tf_op jit(solution)/shard_map/all_gather | solution.py:38
  488.9 0.0 copy-done.1
  488.9 1.8 fusion.27
  490.8 38.6 %all-gather.4 = f32[1,1024,128]{2,1,0:T(8,128)S(1)} all-gather(f32[1,64,128]{2,1,0:T(8,128)S(1)} %dynamic-slice_subtract_fusion.3), channel_id=6, replica_groups=mesh['blk'=16,'grp'=2] {'blk'}, dimensions={1}, use_global_device_ids=true | all-gather | bytes 557056 | tf_op jit(solution)/shard_map/all_gather | solution.py:28
  529.3 0.5 bitcast_dynamic-update-slice_fusion.2
  529.8 40.8 %all_gather.54 = f32[1024,128]{1,0:T(8,128)S(1)} all-gather(f32[64,128]{1,0:T(8,128)S(1)} %get-tuple-element.23), channel_id=1, replica_groups=mesh['blk'=16,'grp'=2] {'blk'}, dimensions={0}, use_global_device_ids=true | all-gather | bytes 557056 | tf_op jit(solution)/shard_map/all_gather | solution.py:38
  570.6 1.8 fusion.30
  572.4 38.6 %all-gather.5 = f32[1,1024,128]{2,1,0:T(8,128)S(1)} all-gather(f32[1,64,128]{2,1,0:T(8,128)S(1)} %dynamic-slice_subtract_fusion.2), channel_id=7, replica_groups=mesh['blk'=16,'grp'=2] {'blk'}, dimensions={1}, use_global_device_ids=true | all-gather | bytes 557056 | tf_op jit(solution)/shard_map/all_gather | solution.py:28
  611.0 0.5 bitcast_dynamic-update-slice_fusion.1
  611.5 40.7 %all_gather.56 = f32[1024,128]{1,0:T(8,128)S(1)} all-gather(f32[64,128]{1,0:T(8,128)S(1)} %get-tuple-element.25), channel_id=1, replica_groups=mesh['blk'=16,'grp'=2] {'blk'}, dimensions={0}, use_global_device_ids=true | all-gather | bytes 557056 | tf_op jit(solution)/shard_map/all_gather | solution.py:38
  652.2 1.8 fusion.33
  654.0 38.4 %all-gather.6 = f32[1,1024,128]{2,1,0:T(8,128)S(1)} all-gather(f32[1,64,128]{2,1,0:T(8,128)S(1)} %dynamic-slice_subtract_fusion.1), channel_id=8, replica_groups=mesh['blk'=16,'grp'=2] {'blk'}, dimensions={1}, use_global_device_ids=true | all-gather | bytes 557056 | tf_op jit(solution)/shard_map/all_gather | solution.py:28
  692.4 0.5 bitcast_dynamic-update-slice_fusion
  692.9 40.3 %all_gather.58 = f32[1024,128]{1,0:T(8,128)S(1)} all-gather(f32[64,128]{1,0:T(8,128)S(1)} %get-tuple-element.27), channel_id=1, replica_groups=mesh['blk'=16,'grp'=2] {'blk'}, dimensions={0}, use_global_device_ids=true | all-gather | bytes 557056 | tf_op jit(solution)/shard_map/all_gather | solution.py:38
  733.2 0.0 copy-start.3
  733.2 0.0 copy-start.4
  733.2 1.8 fusion
  735.0 38.3 %all-gather.7 = f32[1,1024,128]{2,1,0:T(8,128)S(1)} all-gather(f32[1,64,128]{2,1,0:T(8,128)S(1)} %dynamic-slice_subtract_fusion), channel_id=9, replica_groups=mesh['blk'=16,'grp'=2] {'blk'}, dimensions={1}, use_global_device_ids=true | all-gather | bytes 557056 | tf_op jit(solution)/shard_map/all_gather | solution.py:28
  773.3 0.5 fusion.36
  773.7 0.0 copy-done.2
  773.7 0.2 convolution_add_fusion
  774.0 0.0 copy-done.3
  774.0 0.0 copy-done.4
  774.0 1.1 maximum_add_fusion
  (10 shorter events, 0.1 us)
Async XLA Ops:
  7.2 191.0 %copy-start = (f32[8,64,1024]{2,1,0:T(8,128)S(1)}, f32[8,64,1024]{2,1,0:T(8,128)}, u32[]{:S(2)}) copy-start(f32[8,64,1024]{2,1,0:T(8,128)} %param.13) | copy-start | bytes 6291460
  7.2 151.6 %all-reduce.2.cloned.1.call-start = ((), (), s32[]{:S(2)}) async-start(), calls=%async_computation | async-start | bytes 524288 | tf_op jit(solution)/shard_map/psum | solution.py:66
  59.8 38.6 %copy-start.7 = (s32[2,24]{1,0:T(2,128)S(1)}, s32[2,24]{1,0:T(2,128)}, u32[]{:S(2)}) copy-start(s32[2,24]{1,0:T(2,128)} %param.10) | copy-start | bytes 580
  59.8 39.8 %copy-start.6 = (s32[8]{0:T(128)S(1)}, s32[8]{0:T(128)}, u32[]{:S(2)}) copy-start(s32[8]{0:T(128)} %param.11) | copy-start | bytes 100
  98.5 675.3 %copy-start.2 = (f32[2,1024,128]{2,1,0:T(8,128)}, f32[2,1024,128]{2,1,0:T(8,128)S(1)}, u32[]{:S(2)}) copy-start(f32[2,1024,128]{2,1,0:T(8,128)S(1)} %get-tuple-element.3) | copy-start | bytes 3145732
  198.2 44.7 %copy-start.5 = (f32[8,64,128]{2,1,0:T(8,128)S(1)}, f32[8,64,128]{2,1,0:T(8,128)}, u32[]{:S(2)}) copy-start(f32[8,64,128]{2,1,0:T(8,128)} %all-reduce.2.cloned.1.call-done) | copy-start | bytes 786436
  198.2 290.7 %copy-start.1 = (f32[8,8,64,1024]{3,2,1,0:T(8,128)S(1)}, f32[8,8,64,1024]{3,2,1,0:T(8,128)}, u32[]{:S(2)}) copy-start(f32[8,8,64,1024]{3,2,1,0:T(8,128)} %param.12) | copy-start | bytes 50331652
  733.2 40.8 %copy-start.3 = (f32[2,1024,128]{2,1,0:T(8,128)S(1)}, f32[2,1024,128]{2,1,0:T(8,128)}, u32[]{:S(2)}) copy-start(f32[2,1024,128]{2,1,0:T(8,128)} %param.9) | copy-start | bytes 3145732
  733.2 40.8 %copy-start.4 = (f32[2,1000,128]{2,1,0:T(8,128)S(1)}, f32[2,1000,128]{2,1,0:T(8,128)}, u32[]{:S(2)}) copy-start(f32[2,1000,128]{2,1,0:T(8,128)} %slice.42) | copy-start | bytes 3072004
Sparse Core Ops, SparseCore 0:
  99.8 18.6 all-reduce.1
